TPU v7x, 32 devices: a whole 2x2x4 slice. The times are simulated.
32 devices in a mesh: row: 2 (over x), col: 4 (over z), box: 4 (over y, core).
Axes of the slice: x: 2, y: 2, z: 4, core: 2. Of those that a mesh axis runs over, the one named last changes fastest.
Arguments:
- coeffs: bfloat16 [81920, 512], P(('row', 'box'), 'col'), may hold values from -6 to 6
- reflectors: bfloat16 [81920, 256], P(('row', 'box')), may hold values from -0.078125 to 0.078125
- factor: float32 [256, 256], replicated, may hold values from -0.375 to 0.375
- func_exp: float32 [81920], replicated, may hold values from 0.5 to 20
- func_atom: int32 [81920], replicated, may hold values from 0 to 8191, never falling along the last dimension, each value on 1 to 20 neighbouring positions
- atom_pos: float32 [3, 8192], replicated, may hold values from 0 to 1
- point_pos: float32 [3, 128, 128], P(None, ('row', 'col', 'box')), may hold values from 0 to 1
- send_tiles: int32 [8, 8, 2], replicated, may hold values from 0 to 79, as said below
- box_tiles: int32 [128, 16], P(('row', 'col', 'box')), may hold values from 0 to 15, as said below
- box_count: int32 [128], P(('row', 'col', 'box')), may hold values from 1 to 16
Outputs:
- rotated: bfloat16 [81920, 512], P(('row', 'box'), 'col')
- density: float32 [128, 128], P(('row', 'col', 'box'))
Inputs may be any that keep to these rules, and one draw needn't show every extreme that they name: `send_tiles`: for each basis group and box group the 2 tiles are different local tiles of the basis group. `box_tiles`: the 16 slots listed by a box are different. `func_atom`: never falls along the basis functions; every atom carries 1 to 20 functions.
All inputs are finite; a program needn't handle non-finite values.
Results may differ from a plain program's by a relative error of at most 0.015.
Values may be sent and summed in bfloat16 or wider, within the bound.
A program may use at most 128 MiB of HBM per device.

v0:
```python
import math
import jax
import jax.numpy as jnp
from jax import lax
from jax.sharding import PartitionSpec as P

K = 512
TILE = 128


def box_density(arrived, slot_alpha, slot_centre, listed, count, points):
    alpha = slot_alpha[listed]
    centre = slot_centre[:, listed]
    first = points[0][:, None, None] - centre[0][None]
    dist = first * first
    second = points[1][:, None, None] - centre[1][None]
    dist = dist + second * second
    third = points[2][:, None, None] - centre[2][None]
    dist = dist + third * third
    live = jnp.arange(listed.shape[0], dtype=jnp.int32) < count
    phi = jnp.where(live[None, :, None], jnp.exp(-alpha[None] * dist), 0.0).astype(jnp.bfloat16)
    phi = phi.reshape(points.shape[1], -1)
    block = arrived[listed].reshape(-1, arrived.shape[2])
    orbital = jnp.dot(phi, block, preferred_element_type=jnp.float32)
    return jnp.sum(orbital * orbital, 1) / (K * TILE)


def by_blocks(arrived, slot_alpha, slot_centre, lists, counts, points):
    boxes = lists.shape[0]
    width = math.gcd(boxes, 2)
    steps = boxes // width
    lists_blocked = lists.reshape(steps, width, lists.shape[1])
    counts_blocked = counts.reshape(steps, width)
    moved = jnp.moveaxis(points, 1, 0)
    points_blocked = moved.reshape(steps, width, moved.shape[1], moved.shape[2])
    single = jax.vmap(
        lambda listed, count, where: box_density(
            arrived, slot_alpha, slot_centre, listed, count, where
        )
    )

    def one_block(items):
        return single(items[0], items[1], items[2])

    result = lax.map(one_block, (lists_blocked, counts_blocked, points_blocked))
    return result.reshape(boxes, result.shape[2])


def per_device(
    coeffs,
    reflectors,
    factor,
    func_exp,
    func_atom,
    atom_pos,
    point_pos,
    send_tiles,
    box_tiles,
    box_count,
):
    panel_part = jnp.dot(reflectors.T, coeffs, preferred_element_type=jnp.float32)
    panel = lax.psum(panel_part.astype(jnp.bfloat16), ("row", "box")).astype(jnp.float32)
    scaled = jnp.dot(factor, panel, precision=lax.Precision.HIGHEST).astype(jnp.bfloat16)
    rotated = (
        coeffs.astype(jnp.float32) - jnp.dot(reflectors, scaled, preferred_element_type=jnp.float32)
    ).astype(jnp.bfloat16)
    peers = lax.axis_size(("row", "box"))
    group = lax.axis_index(("row", "box"))
    capacity = send_tiles.shape[2]
    local_tiles = coeffs.shape[0] // TILE
    slots = jnp.arange(peers * capacity, dtype=jnp.int32)
    source = slots // capacity
    within = slots % capacity
    tile = source * local_tiles + send_tiles[source, group, within]
    funcs = tile[:, None] * TILE + jnp.arange(TILE, dtype=jnp.int32)[None, :]
    slot_alpha = func_exp[funcs]
    slot_centre = atom_pos[:, func_atom[funcs]]
    outgoing_index = send_tiles[group]
    outgoing = rotated.reshape(local_tiles, TILE, rotated.shape[1])[outgoing_index]
    arrived = lax.all_to_all(outgoing, ("row", "box"), split_axis=0, concat_axis=0, tiled=True)
    arrived = arrived.reshape(peers * capacity, TILE, arrived.shape[3])
    lists, counts = (
        lax.all_gather(box_tiles, "col", axis=0, tiled=True),
        lax.all_gather(box_count, "col", axis=0, tiled=True),
    )
    points = lax.all_gather(point_pos, "col", axis=1, tiled=True)
    partial_value = by_blocks(arrived, slot_alpha, slot_centre, lists, counts, points)
    density = lax.psum_scatter(
        partial_value.astype(jnp.bfloat16), "col", scatter_dimension=0, tiled=True
    ).astype(jnp.float32)
    return (rotated, density)


def solution(mesh):
    in_specs = (
        P(("row", "box"), "col"),
        P(("row", "box"), None),
        P(),
        P(),
        P(),
        P(),
        P(None, ("row", "col", "box"), None),
        P(),
        P(("row", "col", "box"), None),
        P(("row", "col", "box")),
    )
    out_specs = (P(("row", "box"), "col"), P(("row", "col", "box"), None))
    return jax.shard_map(
        per_device, mesh=mesh, in_specs=in_specs, out_specs=out_specs, check_vma=False
    )
```

profile of v0, /device:TPU:0, one launch (start us, length us, event | category | flops | bytes accessed | tf_op | source)
XLA Modules:
  0.0 196.5 jit_solution(6431484893824231304)
XLA Ops:
  7.2 5.5 %convolution_convert_fusion = bf16[256,128]{1,0:T(8,128)(2,1)} fusion(bf16[10240,256]{1,0:T(8,128)(2,1)} %param.13, bf16[10240,128]{1,0:T(8,128)(2,1)} %param.12), kind=kOutput, calls=%fused_computation.42 | convolution fusion | flops 671121408 | bytes 7929856 | tf_op jit(solution)/shard_map/dot_general | solution.py:61
  13.8 3.0 %copy.28 = bf16[10240,128]{0,1:T(8,128)(2,1)S(1)} copy(bf16[10240,128]{1,0:T(8,128)(2,1)} %param.12) | data formatting | bytes 5242880 | tf_op args[0]
  16.8 2.6 %copy.31 = f32[3,8192]{0,1:T(8,128)} copy(f32[3,8192]{1,0:T(4,128)S(1)} %copy-done.5) | data formatting | bytes 196608 | tf_op args[5]
  19.4 48.7 %all-reduce.4.cloned.1.call-done = bf16[256,128]{1,0:T(8,128)(2,1)} async-done(((bf16[256,128]{1,0:T(8,128)(2,1)}), bf16[256,128]{1,0:T(8,128)(2,1)}) %all-reduce.4.cloned.1.call-update) | async-done | bytes 65552 | tf_op jit(solution)/shard_map/psum | solution.py:62
  68.1 1.1 convolution_convert_fusion.1
  69.3 5.8 %fusion.13 = bf16[10240,128]{0,1:T(8,128)(2,1)} fusion(bf16[128,256]{1,0:T(8,128)(2,1)S(1)} %convolution_convert_fusion.1, bf16[10240,256]{1,0:T(8,128)(2,1)} %param.13, bf16[10240,128]{0,1:T(8,128)(2,1)S(1)} %copy.28), kind=kOutput, calls=%fused_computation.41 | convolution fusion | flops 675020800 | bytes 10551296 | tf_op jit(solution)/shard_map/dot_general | solution.py:65
  75.1 3.2 %copy.36 = bf16[10240,128]{1,0:T(8,128)(2,1)S(1)} copy(bf16[10240,128]{0,1:T(8,128)(2,1)} %fusion.13) | data formatting | bytes 5242880
  78.3 1.6 gather_fusion.7
  80.0 3.5 %all-to-all-start = ((bf16[8,2,128,128]{3,2,1,0:T(8,128)(2,1)}), bf16[8,2,128,128]{3,2,1,0:T(8,128)(2,1)S(1)}, u32[]{:S(2)}, u32[]{:S(2)}) async-start(bf16[8,2,128,128]{3,2,1,0:T(8,128)(2,1)} %bitcast.116), calls=%async_computation | async-start | bytes 1048576 | tf_op jit(solution)/shard_map/all_to_all | solution.py:80
  83.6 11.8 %gather_fusion.5 = s32[2048]{0:T(1024)S(1)} fusion(s32[81920]{0:T(1024)S(1)} %copy-done, s32[2048]{0:T(1024)S(1)} %fusion.15), kind=kCustom, calls=%fused_computation.5 | custom fusion | bytes 24576 | tf_op jit(solution)/shard_map/gather | solution.py:77
  95.4 7.7 %gather_fusion.6 = f32[2048,3]{1,0:T(8,128)S(1)} fusion(f32[3,8192]{0,1:T(8,128)} %copy.31, s32[2048]{0:T(1024)S(1)} %fusion.17), kind=kCustom, calls=%fused_computation.6 | custom fusion | bytes 57344 | tf_op jit(solution)/shard_map/gather | solution.py:77
  103.4 11.8 %gather_fusion.4 = f32[2048]{0:T(1024)S(1)} fusion(f32[81920]{0:T(1024)S(1)} %copy-done.1, s32[2048]{0:T(1024)S(1)} %fusion.15), kind=kCustom, calls=%fused_computation.4 | custom fusion | bytes 24576 | tf_op jit(solution)/shard_map/gather | solution.py:76
  116.8 8.3 %all-reduce = s32[16]{0:T(128)S(1)} all-reduce(s32[16]{0:T(128)S(1)} %dynamic-update-slice), channel_id=1, replica_groups=mesh['row'=2,'col'=4,'box'=4] {'col'}, use_global_device_ids=true, to_apply=%add | all-reduce | flops 16 | bytes 128
  125.1 13.1 %all_gather.11 = f32[3,16,128]{2,0,1:T(4,128)S(1)} all-gather(f32[3,4,128]{2,0,1:T(4,128)S(1)} %copy.29), channel_id=1, replica_groups=mesh['row'=2,'col'=4,'box'=4] {'col'}, dimensions={1}, use_global_device_ids=true | all-gather | bytes 30720 | tf_op jit(solution)/shard_map/all_gather | solution.py:86
  138.9 11.9 %all-gather = s32[4,4,16]{2,1,0:T(4,128)S(1)} all-gather(s32[1,4,16]{2,1,0:T(4,128)S(1)} %bitcast.126), channel_id=1, replica_groups=mesh['row'=2,'col'=4,'box'=4] {'col'}, dimensions={0}, use_global_device_ids=true | all-gather | bytes 1280 | tf_op jit(solution)/shard_map/all_gather | solution.py:83
  150.8 29.7 %while.10 = (s32[]{:T(128)}, bf16[8,2,128]{2,1,0:T(2,128)(2,1)S(1)}, s32[8,2]{1,0:T(8,128)S(1)}, s32[8,2,16]{2,1,0:T(2,128)S(1)}, f32[16,128]{1,0:T(8,128)S(1)},...) while((s32[]{:T(128)}, ...), condition=%wide.region_3.4_spmd, body=%wide.region_1.3_spmd.sunk | while | flops 140055680 | bytes 3644613 | solution.py:45
  151.7 0.7 gather_fusion
  153.3 1.2 fusion.41
  155.4 0.7 gather_fusion
  157.0 1.2 fusion.41
  159.1 0.7 gather_fusion
  160.7 1.2 fusion.41
  162.8 0.7 gather_fusion
  164.4 1.2 fusion.41
  166.5 0.7 gather_fusion
  168.1 1.2 fusion.41
  170.3 0.7 gather_fusion
  171.8 1.2 fusion.41
  174.0 0.7 gather_fusion
  175.5 1.2 fusion.41
  179.3 1.2 fusion.41
  180.5 8.6 %all-reduce.1 = bf16[16,128]{1,0:T(8,128)(2,1)S(1)} all-reduce(bf16[16,128]{1,0:T(8,128)(2,1)S(1)} %bitcast.125), channel_id=2, replica_groups=mesh['row'=2,'col'=4,'box'=4] {'col'}, use_global_device_ids=true, to_apply=%region_4.5.clone | all-reduce | flops 2048 | bytes 8192
  (178 shorter events, 17.0 us)
Async XLA Ops:
  7.2 76.4 %copy-start = (s32[81920]{0:T(1024)S(1)}, s32[81920]{0:T(1024)}, u32[]{:S(2)}) copy-start(s32[81920]{0:T(1024)} %param.16) | copy-start | bytes 983044
  7.2 5.7 %copy-start.2 = (s32[8,8,2]{1,2,0:T(2,128)S(1)}, s32[8,8,2]{1,2,0:T(2,128)}, u32[]{:S(2)}) copy-start(s32[8,8,2]{1,2,0:T(2,128)} %param.19) | copy-start | bytes 1540
  7.2 60.9 %all-reduce.4.cloned.1.call-start = ((), (), s32[]{:S(2)}) async-start(), calls=%async_computation.1 | async-start | bytes 131072 | tf_op jit(solution)/shard_map/psum | solution.py:62
  13.7 3.1 %copy-start.5 = (f32[3,8192]{1,0:T(4,128)S(1)}, f32[3,8192]{1,0:T(4,128)}, u32[]{:S(2)}) copy-start(f32[3,8192]{1,0:T(4,128)} %param.17) | copy-start | bytes 294916
  16.8 51.3 %copy-start.4 = (f32[256,256]{1,0:T(8,128)S(1)}, f32[256,256]{1,0:T(8,128)}, u32[]{:S(2)}) copy-start(f32[256,256]{1,0:T(8,128)} %param.14) | copy-start | bytes 786436
  78.3 5.2 %copy-start.3 = (bf16[10240,128]{1,0:T(8,128)(2,1)}, bf16[10240,128]{1,0:T(8,128)(2,1)S(1)}, u32[]{:S(2)}) copy-start(bf16[10240,128]{1,0:T(8,128)(2,1)S(1)} %copy.36) | copy-start | bytes 7864324
  80.0 70.8 %all-to-all-start = ((bf16[8,2,128,128]{3,2,1,0:T(8,128)(2,1)}), bf16[8,2,128,128]{3,2,1,0:T(8,128)(2,1)S(1)}, u32[]{:S(2)}, u32[]{:S(2)}) async-start(bf16[8,2,128,128]{3,2,1,0:T(8,128)(2,1)} %bitcast.116), calls=%async_computation | async-start | bytes 1048576 | tf_op jit(solution)/shard_map/all_to_all | solution.py:80
  95.4 8.1 %copy-start.1 = (f32[81920]{0:T(1024)S(1)}, f32[81920]{0:T(1024)}, u32[]{:S(2)}) copy-start(f32[81920]{0:T(1024)} %param.15) | copy-start | bytes 983044
  103.4 11.8 %copy-start.8 = (u32[32]{0:T(128)S(1)}, u32[32]{0:T(128)}, u32[]{:S(2)}) copy-start(u32[32]{0:T(128)} %constant.107) | copy-start | bytes 388
  103.4 13.1 %copy-start.9 = (s32[4]{0:T(128)S(1)}, s32[4]{0:T(128)}, u32[]{:S(2)}) copy-start(s32[4]{0:T(128)} %param.21) | copy-start | bytes 52
  103.4 21.7 %copy-start.6 = (f32[3,4,128]{2,1,0:T(4,128)S(1)}, f32[3,4,128]{2,1,0:T(4,128)}, u32[]{:S(2)}) copy-start(f32[3,4,128]{2,1,0:T(4,128)} %param.18) | copy-start | bytes 18436
  103.4 35.5 %copy-start.7 = (s32[4,16]{1,0:T(4,128)S(1)}, s32[4,16]{1,0:T(4,128)}, u32[]{:S(2)}) copy-start(s32[4,16]{1,0:T(4,128)} %param.20) | copy-start | bytes 772
Sparse Core Ops, SparseCore 0:
  12.9 55.1 all-reduce.3
where the time goes:
time: 197 us
  local copies, waits for them, and re-layouts  62.4 us (32%)
  waiting for transfers between devices  48.7 us (25%)
  blocking collectives  41.9 us (21%)
  matrix products  22.2 us (11%)
  between operations  15.6 us (8%)
  starting transfers between devices  3.53 us (2%)
    psum x1, waiting for transfers between devices, per_device(): lax.psum(panel_part.astype(jnp.bfloat16), ('row', 'box'))  48.7 us
    gather x3, local copies, waits for them, and re-layouts, per_device(): slot_centre = atom_pos[:, func_atom[funcs]]  19.8 us
    unnamed x2, blocking collectives  16.9 us
    all_gather x1, blocking collectives, per_device(): points = lax.all_gather(point_pos, 'col', axis=1, tiled=True)  13.1 us
    all_gather x1, blocking collectives, per_device(): lax.all_gather(box_tiles, 'col', axis=0, tiled=True)  11.9 us
    gather x1, local copies, waits for them, and re-layouts, per_device(): slot_alpha = func_exp[funcs]  11.8 us
    unnamed x27, local copies, waits for them, and re-layouts  9.83 us
    dot_general x8, matrix products, box_density(): orbital = jnp.dot(phi, block, preferred_element_type=jnp.float32)  9.66 us
  transfers between devices with their start and end apart: 2, of which 1 were waited for; matrix products, arithmetic and copies ran while one was open for 20% of the time, Pallas kernels for 0%

commit v1 on v0

--- a/solution.py
+++ b/solution.py
@@ -58,8 +58,12 @@
     box_tiles,
     box_count,
 ):
+
+    def create_streams(row_data):
+        return lax.psum(lax.psum(row_data, axis_name="box"), "row")
+
     panel_part = jnp.dot(reflectors.T, coeffs, preferred_element_type=jnp.float32)
-    panel = lax.psum(panel_part.astype(jnp.bfloat16), ("row", "box")).astype(jnp.float32)
+    panel = create_streams(panel_part.astype(jnp.bfloat16)).astype(jnp.float32)
     scaled = jnp.dot(factor, panel, precision=lax.Precision.HIGHEST).astype(jnp.bfloat16)
     rotated = (
         coeffs.astype(jnp.float32) - jnp.dot(reflectors, scaled, preferred_element_type=jnp.float32)

time: 197 us -> 199 us (1.010)
    psum x1 -> x2, waiting for transfers between devices: 48.7 us -> 50.3 us  [create_streams(): return lax.psum(lax.psum(row_data, axis_name='box'), 'row')]
  transfers between devices with their start and end apart: 2 -> 3, of which waited for: 1 -> 2; matrix products, arithmetic and copies ran while one was open for 20% -> 20% of each run, Pallas kernels for 0% -> 0%
where the time goes in v1:
time: 199 us; the launch traced here: 198 us
  local copies, waits for them, and re-layouts  62.4 us (31%)
  waiting for transfers between devices  50.4 us (25%)
  blocking collectives  41.9 us (21%)
  matrix products  22.2 us (11%)
  between operations  15.6 us (8%)
  starting transfers between devices  3.57 us (2%)
    psum x2, waiting for transfers between devices, create_streams(): return lax.psum(lax.psum(row_data, axis_name='box'), 'row')  50.3 us
    gather x3, local copies, waits for them, and re-layouts, per_device(): slot_centre = atom_pos[:, func_atom[funcs]]  19.8 us
    unnamed x2, blocking collectives  16.9 us
    all_gather x1, blocking collectives, per_device(): points = lax.all_gather(point_pos, 'col', axis=1, tiled=True)  13.1 us
    all_gather x1, blocking collectives, per_device(): lax.all_gather(box_tiles, 'col', axis=0, tiled=True)  11.9 us
    gather x1, local copies, waits for them, and re-layouts, per_device(): slot_alpha = func_exp[funcs]  11.8 us
    unnamed x27, local copies, waits for them, and re-layouts  9.83 us
    dot_general x8, matrix products, box_density(): orbital = jnp.dot(phi, block, preferred_element_type=jnp.float32)  9.66 us
  transfers between devices with their start and end apart: 3, of which 2 were waited for; matrix products, arithmetic and copies ran while one was open for 20% of the time, Pallas kernels for 0%

profile of v1, /device:TPU:0, one launch (start us, length us, event | category | flops | bytes accessed | tf_op | source)
XLA Modules:
  0.0 198.2 jit_solution(6065969235184828179)
XLA Ops:
  7.2 5.5 %convolution_convert_fusion = bf16[256,128]{1,0:T(8,128)(2,1)} fusion(bf16[10240,256]{1,0:T(8,128)(2,1)} %param.13, bf16[10240,128]{1,0:T(8,128)(2,1)} %param.12), kind=kOutput, calls=%fused_computation.42 | convolution fusion | flops 671121408 | bytes 7929856 | tf_op jit(solution)/shard_map/dot_general | solution.py:65
  13.6 3.0 %copy.28 = bf16[10240,128]{0,1:T(8,128)(2,1)S(1)} copy(bf16[10240,128]{1,0:T(8,128)(2,1)} %param.12) | data formatting | bytes 5242880 | tf_op args[0]
  16.7 2.6 %copy.31 = f32[3,8192]{0,1:T(8,128)} copy(f32[3,8192]{1,0:T(4,128)S(1)} %copy-done.5) | data formatting | bytes 196608 | tf_op args[5]
  19.5 27.2 %all-reduce.5.cloned.1.call-done = bf16[256,128]{1,0:T(8,128)(2,1)} async-done(((bf16[256,128]{1,0:T(8,128)(2,1)}), bf16[256,128]{1,0:T(8,128)(2,1)}) %all-reduce.5.cloned.1.call-update) | async-done | bytes 65552 | tf_op jit(solution)/shard_map/psum | solution.py:63
  46.7 23.1 %all-reduce.7.cloned.1.call-done = bf16[256,128]{1,0:T(8,128)(2,1)} async-done(((bf16[256,128]{1,0:T(8,128)(2,1)}), bf16[256,128]{1,0:T(8,128)(2,1)}) %all-reduce.7.cloned.1.call-update) | async-done | bytes 65552 | tf_op jit(solution)/shard_map/psum | solution.py:63
  69.8 1.1 convolution_convert_fusion.1
  71.0 5.8 %fusion.13 = bf16[10240,128]{0,1:T(8,128)(2,1)} fusion(bf16[128,256]{1,0:T(8,128)(2,1)S(1)} %convolution_convert_fusion.1, bf16[10240,256]{1,0:T(8,128)(2,1)} %param.13, bf16[10240,128]{0,1:T(8,128)(2,1)S(1)} %copy.28), kind=kOutput, calls=%fused_computation.41 | convolution fusion | flops 675020800 | bytes 10551296 | tf_op jit(solution)/shard_map/dot_general | solution.py:69
  76.8 3.2 %copy.36 = bf16[10240,128]{1,0:T(8,128)(2,1)S(1)} copy(bf16[10240,128]{0,1:T(8,128)(2,1)} %fusion.13) | data formatting | bytes 5242880
  80.0 1.6 gather_fusion.7
  81.7 3.5 %all-to-all-start = ((bf16[8,2,128,128]{3,2,1,0:T(8,128)(2,1)}), bf16[8,2,128,128]{3,2,1,0:T(8,128)(2,1)S(1)}, u32[]{:S(2)}, u32[]{:S(2)}) async-start(bf16[8,2,128,128]{3,2,1,0:T(8,128)(2,1)} %bitcast.26), calls=%async_computation | async-start | bytes 1048576 | tf_op jit(solution)/shard_map/all_to_all | solution.py:84
  85.3 11.8 %gather_fusion.5 = s32[2048]{0:T(1024)S(1)} fusion(s32[81920]{0:T(1024)S(1)} %copy-done, s32[2048]{0:T(1024)S(1)} %fusion.15), kind=kCustom, calls=%fused_computation.5 | custom fusion | bytes 24576 | tf_op jit(solution)/shard_map/gather | solution.py:81
  97.1 7.7 %gather_fusion.6 = f32[2048,3]{1,0:T(8,128)S(1)} fusion(f32[3,8192]{0,1:T(8,128)} %copy.31, s32[2048]{0:T(1024)S(1)} %fusion.17), kind=kCustom, calls=%fused_computation.6 | custom fusion | bytes 57344 | tf_op jit(solution)/shard_map/gather | solution.py:81
  105.1 11.8 %gather_fusion.4 = f32[2048]{0:T(1024)S(1)} fusion(f32[81920]{0:T(1024)S(1)} %copy-done.1, s32[2048]{0:T(1024)S(1)} %fusion.15), kind=kCustom, calls=%fused_computation.4 | custom fusion | bytes 24576 | tf_op jit(solution)/shard_map/gather | solution.py:80
  118.5 8.3 %all-reduce = s32[16]{0:T(128)S(1)} all-reduce(s32[16]{0:T(128)S(1)} %dynamic-update-slice), channel_id=1, replica_groups=mesh['row'=2,'col'=4,'box'=4] {'col'}, use_global_device_ids=true, to_apply=%add | all-reduce | flops 16 | bytes 128
  126.8 13.1 %all_gather.11 = f32[3,16,128]{2,0,1:T(4,128)S(1)} all-gather(f32[3,4,128]{2,0,1:T(4,128)S(1)} %copy.29), channel_id=1, replica_groups=mesh['row'=2,'col'=4,'box'=4] {'col'}, dimensions={1}, use_global_device_ids=true | all-gather | bytes 30720 | tf_op jit(solution)/shard_map/all_gather | solution.py:90
  140.6 11.9 %all-gather = s32[4,4,16]{2,1,0:T(4,128)S(1)} all-gather(s32[1,4,16]{2,1,0:T(4,128)S(1)} %bitcast.125), channel_id=1, replica_groups=mesh['row'=2,'col'=4,'box'=4] {'col'}, dimensions={0}, use_global_device_ids=true | all-gather | bytes 1280 | tf_op jit(solution)/shard_map/all_gather | solution.py:87
  152.5 29.7 %while.10 = (s32[]{:T(128)}, bf16[8,2,128]{2,1,0:T(2,128)(2,1)S(1)}, s32[8,2]{1,0:T(8,128)S(1)}, s32[8,2,16]{2,1,0:T(2,128)S(1)}, f32[16,128]{1,0:T(8,128)S(1)},...) while((s32[]{:T(128)}, ...), condition=%wide.region_4.5_spmd, body=%wide.region_2.4_spmd.sunk | while | flops 140055680 | bytes 3644613 | solution.py:45
  155.0 1.2 fusion.41
  158.7 1.2 fusion.41
  160.8 0.7 gather_fusion
  162.4 1.2 fusion.41
  164.5 0.7 gather_fusion
  166.1 1.2 fusion.41
  168.2 0.7 gather_fusion
  169.8 1.2 fusion.41
  172.0 0.7 gather_fusion
  173.5 1.2 fusion.41
  175.7 0.7 gather_fusion
  177.2 1.2 fusion.41
  179.4 0.7 gather_fusion
  181.0 1.2 fusion.41
  182.2 8.6 %all-reduce.1 = bf16[16,128]{1,0:T(8,128)(2,1)S(1)} all-reduce(bf16[16,128]{1,0:T(8,128)(2,1)S(1)} %bitcast.124), channel_id=2, replica_groups=mesh['row'=2,'col'=4,'box'=4] {'col'}, use_global_device_ids=true, to_apply=%region_5.6.clone | all-reduce | flops 2048 | bytes 8192
  (181 shorter events, 17.8 us)
Async XLA Ops:
  7.2 78.1 %copy-start = (s32[81920]{0:T(1024)S(1)}, s32[81920]{0:T(1024)}, u32[]{:S(2)}) copy-start(s32[81920]{0:T(1024)} %param.16) | copy-start | bytes 983044
  7.2 5.7 %copy-start.2 = (s32[8,8,2]{1,2,0:T(2,128)S(1)}, s32[8,8,2]{1,2,0:T(2,128)}, u32[]{:S(2)}) copy-start(s32[8,8,2]{1,2,0:T(2,128)} %param.19) | copy-start | bytes 1540
  7.2 39.5 %all-reduce.5.cloned.1.call-start = ((), (), s32[]{:S(2)}) async-start(), calls=%async_computation.1 | async-start | bytes 131072 | tf_op jit(solution)/shard_map/psum | solution.py:63
  12.8 57.0 %all-reduce.7.cloned.1.call-start = ((), (), s32[]{:S(2)}) async-start(), calls=%async_computation.2 | async-start | bytes 131072 | tf_op jit(solution)/shard_map/psum | solution.py:63
  13.6 3.1 %copy-start.5 = (f32[3,8192]{1,0:T(4,128)S(1)}, f32[3,8192]{1,0:T(4,128)}, u32[]{:S(2)}) copy-start(f32[3,8192]{1,0:T(4,128)} %param.17) | copy-start | bytes 294916
  16.6 53.2 %copy-start.4 = (f32[256,256]{1,0:T(8,128)S(1)}, f32[256,256]{1,0:T(8,128)}, u32[]{:S(2)}) copy-start(f32[256,256]{1,0:T(8,128)} %param.14) | copy-start | bytes 786436
  80.0 1.7 copy-start.3
  81.7 70.8 %all-to-all-start = ((bf16[8,2,128,128]{3,2,1,0:T(8,128)(2,1)}), bf16[8,2,128,128]{3,2,1,0:T(8,128)(2,1)S(1)}, u32[]{:S(2)}, u32[]{:S(2)}) async-start(bf16[8,2,128,128]{3,2,1,0:T(8,128)(2,1)} %bitcast.26), calls=%async_computation | async-start | bytes 1048576 | tf_op jit(solution)/shard_map/all_to_all | solution.py:84
  97.1 8.1 %copy-start.1 = (f32[81920]{0:T(1024)S(1)}, f32[81920]{0:T(1024)}, u32[]{:S(2)}) copy-start(f32[81920]{0:T(1024)} %param.15) | copy-start | bytes 983044
  105.1 11.8 %copy-start.8 = (u32[32]{0:T(128)S(1)}, u32[32]{0:T(128)}, u32[]{:S(2)}) copy-start(u32[32]{0:T(128)} %constant.107) | copy-start | bytes 388
  105.1 13.1 %copy-start.9 = (s32[4]{0:T(128)S(1)}, s32[4]{0:T(128)}, u32[]{:S(2)}) copy-start(s32[4]{0:T(128)} %param.21) | copy-start | bytes 52
  105.1 21.7 %copy-start.6 = (f32[3,4,128]{2,1,0:T(4,128)S(1)}, f32[3,4,128]{2,1,0:T(4,128)}, u32[]{:S(2)}) copy-start(f32[3,4,128]{2,1,0:T(4,128)} %param.18) | copy-start | bytes 18436
  105.1 35.5 %copy-start.7 = (s32[4,16]{1,0:T(4,128)S(1)}, s32[4,16]{1,0:T(4,128)}, u32[]{:S(2)}) copy-start(s32[4,16]{1,0:T(4,128)} %param.20) | copy-start | bytes 772
Sparse Core Ops, SparseCore 0:
  12.9 33.7 all-reduce.4
  49.0 20.7 all-reduce.6
